TPU v7x, 32 devices: a whole 2x2x4 slice. The times are simulated.
32 devices in a mesh: dp: 8 (over z, y), seq: 4 (over x, core).
Axes of the slice: x: 2, y: 2, z: 4, core: 2. Of those that a mesh axis runs over, the one named last changes fastest.
Arguments:
- tokens: bfloat16 [16, 2048, 768], P('dp', 'seq'), may hold values from -6 to 6
- first_values: bfloat16 [16, 2048, 384], P('dp', 'seq'), may hold values from -6 to 6
- cotangent: bfloat16 [16, 2048, 768], P('dp', 'seq'), may hold values from -6 to 6
- lengths: int32 [16], P('dp'), may hold values from 64 to 2048, as said below
- master_tiles: float32 [416, 128, 128], P(('dp', 'seq'))
- left_stat: float32 [416, 128, 128], P(('dp', 'seq'))
- right_stat: float32 [416, 128, 128], P(('dp', 'seq'))
- left_root: float32 [416, 128, 128], P(('dp', 'seq'))
- right_root: float32 [416, 128, 128], P(('dp', 'seq'))
- vector_params: float32 [8832], replicated
- vector_stat: float32 [8832], replicated
Outputs:
- block_output: bfloat16 [16, 2048, 768], P('dp', 'seq')
- tokens_grad: float32 [16, 2048, 768], P('dp', 'seq')
- first_values_grad: float32 [16, 2048, 384], P('dp', 'seq')
- tile_grads: float32 [416, 128, 128], P(('dp', 'seq'))
- left_new: float32 [416, 128, 128], P(('dp', 'seq'))
- right_new: float32 [416, 128, 128], P(('dp', 'seq'))
- tiles_new: float32 [416, 128, 128], P(('dp', 'seq'))
- vector_grads: float32 [8832], replicated
- vector_stat_new: float32 [8832], replicated
- vector_new: float32 [8832], replicated
- grad_norm: float32 [], replicated
Inputs may be any that keep to these rules, and one draw needn't show every extreme that they name: `lengths`: each sequence's length; in every draw some sequence has exactly 2048.
All inputs are finite; a program needn't handle non-finite values.
Results may differ from a plain program's by a relative error of at most 0.012.
The roundings to bfloat16 on the way count: a program that leaves them out, or rounds other values in their place, can miss the bound.
Values may be sent and summed in bfloat16 or wider, within the bound.
A program may use at most 192 MiB of HBM per device.

v0:
```python
import jax
import jax.numpy as jnp
from jax import lax
from jax.sharding import PartitionSpec as P

D = 768
HD = 64
FF = 3072
VW = 384
QBLK = 512
TILE = 128
CLIP = 256
highest = lax.Precision.HIGHEST
norm_eps = 1e-05
clip_eps = 1e-06
decay_rate = 0.5
matrix_rate = 0.3
vector_rate = 0.1
moment_eps = 1e-08
masked_score = -1e30


def matrix_shapes():
    return ((D, D), (D, D), (D, VW), (D, D), (D, FF), (FF, D))


def untile(stacked, row_count, col_count):
    shaped = stacked.reshape(row_count // TILE, col_count // TILE, TILE, TILE)
    return shaped.transpose(0, 2, 1, 3).reshape(row_count, col_count)


def retile(matrix):
    row_count, col_count = matrix.shape
    shaped = matrix.reshape(row_count // TILE, TILE, col_count // TILE, TILE)
    return shaped.transpose(0, 2, 1, 3).reshape(-1, TILE, TILE)


def split_tiles(stacked):
    matrices = []
    offset = 0
    for row_count, col_count in matrix_shapes():
        amount = row_count // TILE * (col_count // TILE)
        matrices.append(untile(stacked[offset : offset + amount], row_count, col_count))
        offset = offset + amount
    return matrices


def join_tiles(matrices, total_tiles):
    joined = jnp.concatenate([retile(matrix) for matrix in matrices], axis=0)
    padding = jnp.zeros((total_tiles - joined.shape[0], TILE, TILE), joined.dtype)
    return jnp.concatenate([joined, padding], axis=0)


def split_vector(vector):
    pieces = []
    offset = 0
    for length in (D, D, D, D, D, D, D, VW, FF):
        pieces.append(vector[offset : offset + length])
        offset = offset + length
    return pieces


def matmul(left_in, right_in):
    return jnp.dot(left_in, right_in, preferred_element_type=jnp.float32)


def contract_rows(left_in, right_in):
    return lax.dot_general(
        left_in, right_in, (((0,), (0,)), ((), ())), preferred_element_type=jnp.float32
    )


def contract_cols(left_in, right_in):
    return lax.dot_general(
        left_in, right_in, (((1,), (1,)), ((), ())), preferred_element_type=jnp.float32
    )


def norm_forward(values, gain_row, shift_row):
    centered = values - jnp.mean(values, axis=-1, keepdims=True)
    variance = jnp.mean(centered * centered, axis=-1, keepdims=True)
    inv_std = lax.rsqrt(variance + norm_eps)
    unit_rows = centered * inv_std
    return (unit_rows * gain_row + shift_row, unit_rows, inv_std)


def norm_backward(grad_in, unit_rows, inv_std, gain_row):
    scaled = grad_in * gain_row
    term = (
        scaled
        - jnp.mean(scaled, axis=-1, keepdims=True)
        - unit_rows * jnp.mean(scaled * unit_rows, axis=-1, keepdims=True)
    )
    return (term * inv_std, jnp.sum(grad_in * unit_rows, axis=0), jnp.sum(grad_in, axis=0))


def allowed_keys(block_index, length, key_count):
    query_pos = block_index * QBLK + jnp.arange(QBLK, dtype=jnp.int32)
    key_pos = jnp.arange(key_count, dtype=jnp.int32)
    return (key_pos[None, :] <= query_pos[:, None]) & (key_pos[None, :] < length)


def attend_forward(inputs):
    query_seq, key_seq, value_seq, length = inputs
    key_count = query_seq.shape[0]
    head_count = query_seq.shape[1] // HD
    query_heads = query_seq.reshape(key_count, head_count, HD)
    key_heads = key_seq.reshape(key_count, head_count, HD)
    value_heads = value_seq.reshape(key_count, head_count, HD)
    score_scale = HD ** (-0.5)

    def one_block(block_index):
        query_rows = lax.dynamic_slice_in_dim(query_heads, block_index * QBLK, QBLK, 0)
        scores = (
            jnp.einsum("qhd,khd->hqk", query_rows, key_heads, preferred_element_type=jnp.float32)
            * score_scale
        )
        scores = jnp.where(allowed_keys(block_index, length, key_count)[None], scores, masked_score)
        top_score = jnp.max(scores, axis=-1, keepdims=True)
        exponent = jnp.exp(scores - top_score)
        totals = jnp.sum(exponent, axis=-1, keepdims=True)
        weights = (exponent / totals).astype(jnp.bfloat16)
        attended = jnp.einsum(
            "hqk,khd->qhd", weights, value_heads, preferred_element_type=jnp.float32
        )
        return (attended.astype(jnp.bfloat16), (top_score + jnp.log(totals))[..., 0])

    attended, log_sums = lax.map(one_block, jnp.arange(key_count // QBLK, dtype=jnp.int32))
    return (
        attended.reshape(key_count, head_count * HD),
        log_sums.transpose(1, 0, 2).reshape(head_count, key_count),
    )


def attend_backward(inputs):
    query_seq, key_seq, value_seq, grad_seq, log_sums, length = inputs
    key_count = query_seq.shape[0]
    head_count = query_seq.shape[1] // HD
    query_heads = query_seq.reshape(key_count, head_count, HD)
    key_heads = key_seq.reshape(key_count, head_count, HD)
    value_heads = value_seq.reshape(key_count, head_count, HD)
    grad_heads = grad_seq.reshape(key_count, head_count, HD)
    score_scale = HD ** (-0.5)

    def one_block(carried, block_index):
        key_acc, value_acc = carried
        query_rows = lax.dynamic_slice_in_dim(query_heads, block_index * QBLK, QBLK, 0)
        grad_rows = lax.dynamic_slice_in_dim(grad_heads, block_index * QBLK, QBLK, 0)
        sums_rows = lax.dynamic_slice_in_dim(log_sums, block_index * QBLK, QBLK, 1)
        scores = (
            jnp.einsum("qhd,khd->hqk", query_rows, key_heads, preferred_element_type=jnp.float32)
            * score_scale
        )
        scores = jnp.where(allowed_keys(block_index, length, key_count)[None], scores, masked_score)
        probs = jnp.exp(scores - sums_rows[..., None])
        probs_grad = jnp.einsum(
            "qhd,khd->hqk", grad_rows, value_heads, preferred_element_type=jnp.float32
        )
        delta = jnp.sum(probs * probs_grad, axis=-1, keepdims=True)
        score_grad = (probs * (probs_grad - delta)).astype(jnp.bfloat16)
        query_grad = (
            jnp.einsum("hqk,khd->qhd", score_grad, key_heads, preferred_element_type=jnp.float32)
            * score_scale
        )
        key_acc = (
            key_acc
            + jnp.einsum("hqk,qhd->khd", score_grad, query_rows, preferred_element_type=jnp.float32)
            * score_scale
        )
        value_acc = value_acc + jnp.einsum(
            "hqk,qhd->khd",
            probs.astype(jnp.bfloat16),
            grad_rows,
            preferred_element_type=jnp.float32,
        )
        return ((key_acc, value_acc), query_grad.astype(jnp.bfloat16))

    zero_acc = jnp.zeros((key_count, head_count, HD), jnp.float32)
    (key_acc, value_acc), query_grad = lax.scan(
        one_block, (zero_acc, zero_acc), jnp.arange(key_count // QBLK, dtype=jnp.int32)
    )
    local_width = head_count * HD
    return (
        query_grad.reshape(key_count, local_width),
        key_acc.astype(jnp.bfloat16).reshape(key_count, local_width),
        value_acc.astype(jnp.bfloat16).reshape(key_count, local_width),
    )


def per_device(
    tokens,
    first_values,
    cotangent,
    lengths,
    master_tiles,
    left_stat,
    right_stat,
    left_root,
    right_root,
    vector_params,
    vector_stat,
):
    seq_count, block_len, model_width = tokens.shape
    gathered = lax.all_gather(master_tiles.astype(jnp.bfloat16), ("dp", "seq"), axis=0, tiled=True)
    w_query, w_key, w_value, w_out, w_hidden, w_proj = split_tiles(gathered)
    (
        gain_one,
        shift_one,
        gain_two,
        shift_two,
        query_bias,
        out_bias,
        proj_bias,
        value_bias,
        hidden_bias,
    ) = split_vector(vector_params)
    flat_tokens = tokens.reshape(-1, model_width).astype(jnp.float32)
    normed_one, unit_one, inv_one = norm_forward(flat_tokens, gain_one, shift_one)
    normed_one = normed_one.astype(jnp.bfloat16)
    queries = (matmul(normed_one, w_query) + query_bias).astype(jnp.bfloat16)
    keys_all = matmul(normed_one, w_key).astype(jnp.bfloat16)
    fresh = (matmul(normed_one, w_value) + value_bias).astype(jnp.bfloat16)
    values_all = jnp.concatenate([fresh, first_values.reshape(-1, VW)], axis=-1)
    packed = jnp.stack([queries, keys_all, values_all]).reshape(
        3, seq_count, block_len, model_width
    )
    head_data = lax.all_to_all(packed, "seq", split_axis=3, concat_axis=2, tiled=True)
    attn_heads, log_sums = lax.map(
        attend_forward, (head_data[0], head_data[1], head_data[2], lengths)
    )
    returned = lax.all_to_all(attn_heads, "seq", split_axis=1, concat_axis=2, tiled=True)
    attended = returned.reshape(-1, model_width)
    residual = flat_tokens + matmul(attended, w_out) + out_bias
    normed_two, unit_two, inv_two = norm_forward(residual, gain_two, shift_two)
    normed_two = normed_two.astype(jnp.bfloat16)
    hidden = matmul(normed_two, w_hidden) + hidden_bias
    active = jax.nn.gelu(hidden, approximate=True).astype(jnp.bfloat16)
    output = residual + matmul(active, w_proj) + proj_bias
    block_output = output.astype(jnp.bfloat16).reshape(tokens.shape)
    positions = lax.axis_index("seq") * block_len + jnp.arange(block_len, dtype=jnp.int32)
    live = positions[None, :] < lengths[:, None]
    out_grad = jnp.where(live[:, :, None], cotangent, jnp.zeros_like(cotangent)).reshape(
        -1, model_width
    )
    grad_w_proj = contract_rows(active, out_grad)
    proj_bias_grad = jnp.sum(out_grad.astype(jnp.float32), axis=0)
    active_grad = contract_cols(out_grad, w_proj)
    gelu_value, gelu_back = jax.vjp(lambda inner: jax.nn.gelu(inner, approximate=True), hidden)
    hidden_grad = gelu_back(active_grad)[0].astype(jnp.bfloat16)
    grad_w_hidden = contract_rows(normed_two, hidden_grad)
    hidden_bias_grad = jnp.sum(hidden_grad.astype(jnp.float32), axis=0)
    norm_two_in = contract_cols(hidden_grad, w_hidden)
    resid_part, gain_two_grad, shift_two_grad = norm_backward(
        norm_two_in, unit_two, inv_two, gain_two
    )
    residual_grad = out_grad.astype(jnp.float32) + resid_part
    branch_grad = residual_grad.astype(jnp.bfloat16)
    grad_w_out = contract_rows(attended, branch_grad)
    out_bias_grad = jnp.sum(branch_grad.astype(jnp.float32), axis=0)
    attended_grad = contract_cols(branch_grad, w_out).astype(jnp.bfloat16)
    grad_heads = lax.all_to_all(
        attended_grad.reshape(seq_count, block_len, model_width),
        "seq",
        split_axis=2,
        concat_axis=1,
        tiled=True,
    )
    query_grad, key_grad, value_grad = lax.map(
        attend_backward, (head_data[0], head_data[1], head_data[2], grad_heads, log_sums, lengths)
    )
    sent_back = lax.all_to_all(
        jnp.stack([query_grad, key_grad, value_grad]),
        "seq",
        split_axis=2,
        concat_axis=3,
        tiled=True,
    )
    queries_grad = sent_back[0].reshape(-1, model_width)
    keys_grad = sent_back[1].reshape(-1, model_width)
    values_grad = sent_back[2].reshape(-1, model_width)
    fresh_grad = values_grad[:, :VW]
    first_grad = values_grad[:, VW:].astype(jnp.float32).reshape(first_values.shape)
    grad_w_query = contract_rows(normed_one, queries_grad)
    grad_w_key = contract_rows(normed_one, keys_grad)
    grad_w_value = contract_rows(normed_one, fresh_grad)
    query_bias_grad = jnp.sum(queries_grad.astype(jnp.float32), axis=0)
    value_bias_grad = jnp.sum(fresh_grad.astype(jnp.float32), axis=0)
    norm_one_in = (
        contract_cols(queries_grad, w_query)
        + contract_cols(keys_grad, w_key)
        + contract_cols(fresh_grad, w_value)
    )
    token_part, gain_one_grad, shift_one_grad = norm_backward(
        norm_one_in, unit_one, inv_one, gain_one
    )
    tokens_grad = (residual_grad + token_part).reshape(tokens.shape)
    grad_stack = join_tiles(
        [grad_w_query, grad_w_key, grad_w_value, grad_w_out, grad_w_hidden, grad_w_proj],
        gathered.shape[0],
    )
    vector_local = jnp.concatenate(
        [
            gain_one_grad,
            shift_one_grad,
            gain_two_grad,
            shift_two_grad,
            query_bias_grad,
            out_bias_grad,
            proj_bias_grad,
            value_bias_grad,
            hidden_bias_grad,
        ]
    )
    owned = lax.psum_scatter(grad_stack, ("dp", "seq"), scatter_dimension=0, tiled=True)
    summed_vector, owned_square = lax.psum((vector_local, jnp.sum(owned * owned)), ("dp", "seq"))
    grad_norm = jnp.sqrt(owned_square + jnp.sum(summed_vector * summed_vector))
    factor = jnp.minimum(1.0, CLIP / (grad_norm + clip_eps))
    clipped = owned * factor
    left_gram = jnp.einsum("tij,tkj->tik", clipped, clipped, precision=highest)
    right_gram = jnp.einsum("tji,tjk->tik", clipped, clipped, precision=highest)
    inner = jnp.einsum("tij,tjk->tik", clipped, right_root, precision=highest)
    step = jnp.einsum("tij,tjk->tik", left_root, inner, precision=highest)
    left_new = decay_rate * left_stat + (1.0 - decay_rate) * left_gram
    right_new = decay_rate * right_stat + (1.0 - decay_rate) * right_gram
    tiles_new = master_tiles - matrix_rate * step
    vector_grads = summed_vector * factor
    vector_stat_new = decay_rate * vector_stat + (1.0 - decay_rate) * vector_grads * vector_grads
    vector_new = vector_params - vector_rate * vector_grads / (
        jnp.sqrt(vector_stat_new) + moment_eps
    )
    return (
        block_output,
        tokens_grad,
        first_grad,
        clipped,
        left_new,
        right_new,
        tiles_new,
        vector_grads,
        vector_stat_new,
        vector_new,
        grad_norm,
    )


def solution(mesh):
    in_specs = (
        P("dp", "seq", None),
        P("dp", "seq", None),
        P("dp", "seq", None),
        P("dp"),
        P(("dp", "seq"), None, None),
        P(("dp", "seq"), None, None),
        P(("dp", "seq"), None, None),
        P(("dp", "seq"), None, None),
        P(("dp", "seq"), None, None),
        P(),
        P(),
    )
    out_specs = (
        P("dp", "seq", None),
        P("dp", "seq", None),
        P("dp", "seq", None),
        P(("dp", "seq"), None, None),
        P(("dp", "seq"), None, None),
        P(("dp", "seq"), None, None),
        P(("dp", "seq"), None, None),
        P(),
        P(),
        P(),
        P(),
    )
    return jax.shard_map(
        per_device, mesh=mesh, in_specs=in_specs, out_specs=out_specs, check_vma=False
    )
```

profile of v0, /device:TPU:0, one launch (start us, length us, event | category | flops | bytes accessed | tf_op | source)
XLA Modules:
  0.0 1392.7 jit_solution(12912429408049028219)
XLA Ops:
  17.5 97.4 %all-gather.2.cloned.1.call-done = bf16[416,128,128]{2,1,0:T(8,128)(2,1)} async-done(((bf16[13,128,128]{2,1,0:T(8,128)(2,1)}), bf16[416,128,128]{2,1,0:T(8,128)(2,1)}) %all-gather.2.cloned.1.call-update) | async-done | bytes 13631504 | tf_op jit(solution)/shard_map/all_gather | solution.py:204
  143.5 13.7 maximum_maximum_fusion
  163.1 53.2 %all-to-all-done = bf16[3,2,512,768]{2,1,0,3:T(2,128)(2,1)} async-done(((bf16[3,2,512,768]{2,1,0,3:T(2,128)(2,1)}), bf16[3,2,512,768]{2,1,0,3:T(2,128)(2,1)}, u32[]{:S(2)}, u32[]{:S(2)}) %all-to-all-start) | async-done | bytes 4718624 | tf_op jit(solution)/shard_map/all_to_all | solution.py:227
  242.3 197.6 %while.54 = (s32[]{:T(128)}, bf16[2,2048,192]{1,2,0:T(8,128)(2,1)}, f32[2,3,2048]{2,1,0:T(4,128)S(1)}, bf16[2,2048,192]{1,2,0:T(8,128)(2,1)}, bf16[2,2048,192]{1...) while((s32[]{:T(128)}, bf16[2,2048,192]{1,2,0:T(8,128)(2,1)}, ...), condition=%wide.region_7.8_spmd, body=%wide.region_2.7_spmd.sunk | while | flops 845251584 | bytes 53479908 | solution.py:228
  246.7 92.3 %while.57 = (s32[]{:T(128)}, bf16[4,512,3,64]{1,3,2,0:T(8,128)(2,1)S(1)}, f32[4,3,512]{2,1,0:T(4,128)S(1)}, s32[4]{0:T(128)S(1)}, s32[]{:T(128)}, /*index=5*/bf1...) while((s32[]{:T(128)}, ...), condition=%wide.region_6.6_spmd, body=%wide.region_3.5_spmd.sunk | while | flops 845251584 | bytes 43976908 | solution.py:128
  345.3 92.3 %while.57 = (s32[]{:T(128)}, bf16[4,512,3,64]{1,3,2,0:T(8,128)(2,1)S(1)}, f32[4,3,512]{2,1,0:T(4,128)S(1)}, s32[4]{0:T(128)S(1)}, s32[]{:T(128)}, /*index=5*/bf1...) while((s32[]{:T(128)}, ...), condition=%wide.region_6.6_spmd, body=%wide.region_3.5_spmd.sunk | while | flops 845251584 | bytes 43976908 | solution.py:128
  453.6 9.1 fusion.122
  479.3 10.4 copy.226
  495.2 22.7 %fusion.54 = (bf16[3072,1024]{0,1:T(8,128)(2,1)}, f32[1024,3072]{1,0:T(8,128)}) fusion(f32[3072]{0:T(1024)S(1)} %copy-done.64, bf16[96,8,24,128]{3,2,1,0:T(8,128)(2,1)S(1)} %bitcast.413, f32[1024,768]{1,0:T(8,128)S(1)} %get-tuple-element.458, f32[768]{0:T(1024)S(1)} %copy-done.51, f32[768]{0:T(1024)S(1)} %copy-done.49, f32[1024]{0:T(1024)S(1)} %add_rsqrt_fusion, ...), kind=kOutput, calls=%fused_computation.81 | convolution fusion | flops 4867227648 | bytes 26765312 | tf_op jit(solution)/shard_map/dot_general | solution.py:64
  517.9 15.1 %convert_reduce_fusion = (f32[3072]{0:T(1024)}, bf16[1024,3072]{1,0:T(8,128)(2,1)S(1)}) fusion(f32[1024,3072]{1,0:T(8,128)} %get-tuple-element.462, f32[3072]{0:T(1024)S(1)} %copy-done.64, bf16[1024,768]{1,0:T(8,128)(2,1)S(1)} %bitcast.391, bf16[96,8,24,128]{3,2,1,0:T(8,128)(2,1)S(1)} %bitcast.410), kind=kOutput, calls=%fused_computation.82 | convolution fusion | flops 4904186880 | bytes 25190400 | tf_op jit(solution)/shard_map/dot_general | solution.py:74
  556.1 8.6 copy.261
  564.7 8.7 all-to-all-done.2
  579.3 277.4 %while.56 = (s32[]{:T(128)}, bf16[2,2048,192]{1,2,0:T(8,128)(2,1)}, bf16[2,2048,192]{1,2,0:T(8,128)(2,1)}, bf16[2,2048,192]{1,2,0:T(8,128)(2,1)}, bf16[2,2048,19...) while((s32[]{:T(128)}, bf16[2,2048,192]{1,2,0:T(8,128)(2,1)}, ...), condition=%wide.region_16.17_spmd, body=%wide.region_12.16_spmd.sunk | while | flops 2065499136 | bytes 171613168 | solution.py:268
  586.7 121.9 %while.58 = (s32[]{:T(128)}, f32[2048,3,64]{0,2,1:T(8,128)S(1)}, f32[2048,3,64]{0,2,1:T(8,128)}, bf16[4,512,3,64]{1,3,2,0:T(8,128)(2,1)}, s32[4]{0:T(128)S(1)}, ...) while((s32[]{:T(128)}, f32[2048,3,64]{0,2,1:T(8,128)S(1)}, ...), condition=%wide.region_15.15_spmd.clone, body=%wide.region_13.14_spmd.clone.sunk | while | flops 2064712704 | bytes 114546992 | solution.py:179
  725.1 121.9 %while.58 = (s32[]{:T(128)}, f32[2048,3,64]{0,2,1:T(8,128)S(1)}, f32[2048,3,64]{0,2,1:T(8,128)}, bf16[4,512,3,64]{1,3,2,0:T(8,128)(2,1)}, s32[4]{0:T(128)S(1)}, ...) while((s32[]{:T(128)}, f32[2048,3,64]{0,2,1:T(8,128)S(1)}, ...), condition=%wide.region_15.15_spmd.clone, body=%wide.region_13.14_spmd.clone.sunk | while | flops 2064712704 | bytes 114546992 | solution.py:179
  873.5 11.7 pad_maximum_fusion
  890.6 8.9 convolution_bitcast_fusion
  915.1 9.3 fusion.133
  924.4 36.8 %all-to-all-done.3 = bf16[3,2,2048,192]{3,1,0,2:T(2,128)(2,1)} async-done(((bf16[3,2,2048,192]{3,1,0,2:T(2,128)(2,1)}), bf16[3,2,2048,192]{3,1,0,2:T(2,128)(2,1)}, u32[]{:S(2)}, u32[]{:S(2)}) %all-to-all-start.3) | async-done | bytes 4718624 | tf_op jit(solution)/shard_map/all_to_all | solution.py:271
  961.2 16.2 %copy.237 = bf16[3,2,4,512,192]{3,4,2,1,0:T(8,128)(2,1)} copy(bf16[3,2,4,512,192]{4,1,0,3,2:T(2,128)(2,1)} %bitcast.49) | data formatting | bytes 9437184 | tf_op jit(solution)/shard_map/all_to_all | solution.py:271
  1020.7 8.6 constant_dynamic-update-slice_fusion.5
  1032.4 14.6 %add_convert_fusion = bf16[1024,768]{1,0:T(8,128)(2,1)} fusion(f32[1024,768]{1,0:T(8,128)} %copy-done.6, bf16[96,8,24,128]{3,2,1,0:T(8,128)(2,1)} %bitcast.407, f32[1024,3072]{1,0:T(8,128)} %get-tuple-element.462, f32[3072]{0:T(1024)S(1)} %copy-done.65, f32[768]{0:T(1024)S(1)} %copy-done.67), kind=kOutput, calls=%fused_computation.130 | convolution fusion | flops 4865654784 | bytes 22035456 | tf_op jit(solution)/shard_map/dot_general | solution.py:64
  1049.2 268.4 %reduce-scatter.2.cloned.1.call-done = f32[13,128,128]{2,1,0:T(8,128)} async-done(((f32[416,128,128]{2,1,0:T(8,128)}), f32[13,128,128]{2,1,0:T(8,128)}) %reduce-scatter.2.cloned.1.call-update) | async-done | bytes 851984 | tf_op jit(solution)/shard_map/reduce_scatter | solution.py:314
  1322.8 46.8 %all-reduce = (f32[]{:T(128)}, f32[8832]{0:T(1024)S(1)}) all-reduce(f32[]{:T(128)} %multiply_reduce_fusion.6, f32[8832]{0:T(1024)S(1)} %constant_dynamic-update-slice_fusion.12), channel_id=1, replica_groups=mesh['dp'=8,'seq'=4] {'dp','seq'}, use_global_device_ids=true, to_apply=%region_21.22 | all-reduce | flops 8833 | bytes 70664 | tf_op jit(solution)/shard_map/psum | solution.py:315
  (543 shorter events, 701.5 us)
Async XLA Ops:
  7.2 1365.1 %copy-start = (f32[13,128,128]{2,1,0:T(8,128)S(1)}, f32[13,128,128]{2,1,0:T(8,128)}, u32[]{:S(2)}) copy-start(f32[13,128,128]{2,1,0:T(8,128)} %param.27) | copy-start | bytes 2555908
  7.2 107.7 %all-gather.2.cloned.1.call-start = ((), (), s32[]{:S(2)}) async-start(), calls=%async_computation.5 | async-start | bytes 14057472 | tf_op jit(solution)/shard_map/all_gather | solution.py:204
  157.3 59.0 %all-to-all-start = ((bf16[3,2,512,768]{2,1,0,3:T(2,128)(2,1)}), bf16[3,2,512,768]{2,1,0,3:T(2,128)(2,1)}, u32[]{:S(2)}, u32[]{:S(2)}) async-start(bf16[3,2,512,768]{2,1,0,3:T(2,128)(2,1)} %maximum_maximum_fusion), calls=%async_computation | async-start | bytes 9437184 | tf_op jit(solution)/shard_map/all_to_all | solution.py:227
  445.9 32.1 %all-to-all-start.1 = ((bf16[2,2048,192]{2,0,1:T(2,128)(2,1)}), bf16[2,2048,192]{2,0,1:T(2,128)(2,1)S(1)}, u32[]{:S(2)}, u32[]{:S(2)}) async-start(bf16[2,2048,192]{2,0,1:T(2,128)(2,1)} %copy.225), calls=%async_computation.1 | async-start | bytes 4194304 | tf_op jit(solution)/shard_map/all_to_all | solution.py:231
  479.3 12.4 copy-start.4
  479.3 12.4 copy-start.68
  493.4 45.8 %copy-start.6 = (f32[1024,768]{1,0:T(8,128)}, f32[1024,768]{1,0:T(8,128)S(1)}, u32[]{:S(2)}) copy-start(f32[1024,768]{1,0:T(8,128)S(1)} %get-tuple-element.458) | copy-start | bytes 9437188
  493.5 45.8 %copy-start.43 = (f32[1024]{0:T(1024)}, f32[1024]{0:T(1024)S(1)}, u32[]{:S(2)}) copy-start(f32[1024]{0:T(1024)S(1)} %broadcast_multiply_fusion.6) | copy-start | bytes 12292
  493.5 24.4 %slice-start.5 = ((s8[4718592]{0:T(1024)(128)(4,1)}), s8[4194304]{0:T(1024)(128)(4,1)S(1)}, s32[]{:S(2)}) async-start(s8[4718592]{0:T(1024)(128)(4,1)} %bitcast.408), calls=%async_computation.12 | async-start | bytes 8388608
  494.1 45.2 %copy-start.45 = (f32[1024]{0:T(1024)}, f32[1024]{0:T(1024)S(1)}, u32[]{:S(2)}) copy-start(f32[1024]{0:T(1024)S(1)} %add_rsqrt_fusion) | copy-start | bytes 12292
  495.2 22.7 %copy-start.10 = (bf16[2,512,768]{2,1,0:T(8,128)(2,1)S(1)}, bf16[2,512,768]{2,1,0:T(8,128)(2,1)}, u32[]{:S(2)}) copy-start(bf16[2,512,768]{2,1,0:T(8,128)(2,1)} %get-tuple-element.419) | copy-start | bytes 4718596
  495.2 22.7 %slice-start.6 = ((s8[4718592]{0:T(1024)(128)(4,1)}), s8[524288]{0:T(1024)(128)(4,1)S(1)}, s32[]{:S(2)}) async-start(s8[4718592]{0:T(1024)(128)(4,1)} %bitcast.408), calls=%async_computation.13 | async-start | bytes 1048576
  548.9 24.5 %all-to-all-start.2 = ((bf16[2,512,768]{1,0,2:T(2,128)(2,1)}), bf16[2,512,768]{1,0,2:T(2,128)(2,1)}, u32[]{:S(2)}, u32[]{:S(2)}) async-start(bf16[2,512,768]{1,0,2:T(2,128)(2,1)} %copy.230), calls=%async_computation.2 | async-start | bytes 3145728 | tf_op jit(solution)/shard_map/all_to_all | solution.py:261
  885.2 76.0 %all-to-all-start.3 = ((bf16[3,2,2048,192]{3,1,0,2:T(2,128)(2,1)}), bf16[3,2,2048,192]{3,1,0,2:T(2,128)(2,1)}, u32[]{:S(2)}, u32[]{:S(2)}) async-start(bf16[3,2,2048,192]{3,1,0,2:T(2,128)(2,1)} %pad_maximum_fusion), calls=%async_computation.3 | async-start | bytes 12582912 | tf_op jit(solution)/shard_map/all_to_all | solution.py:271
  890.5 427.1 %reduce-scatter.2.cloned.1.call-start = ((), (), s32[]{:S(2)}) async-start(), calls=%async_computation.6 | async-start | bytes 28114944 | tf_op jit(solution)/shard_map/reduce_scatter | solution.py:314
  1032.4 16.5 %copy-start.70 = (f32[768]{0:T(1024)S(1)}, f32[768]{0:T(1024)}, u32[]{:S(2)}) copy-start(f32[768]{0:T(1024)} %get-tuple-element.333) | copy-start | bytes 9220
  1032.4 16.5 %copy-start.69 = (f32[768]{0:T(1024)S(1)}, f32[768]{0:T(1024)}, u32[]{:S(2)}) copy-start(f32[768]{0:T(1024)} %get-tuple-element.339) | copy-start | bytes 9220
  1032.4 16.5 %copy-start.61 = (f32[768]{0:T(1024)S(1)}, f32[768]{0:T(1024)}, u32[]{:S(2)}) copy-start(f32[768]{0:T(1024)} %get-tuple-element.420) | copy-start | bytes 9220
  1032.4 16.5 %copy-start.60 = (f32[768]{0:T(1024)S(1)}, f32[768]{0:T(1024)}, u32[]{:S(2)}) copy-start(f32[768]{0:T(1024)} %get-tuple-element.418) | copy-start | bytes 9220
  1032.4 16.7 %copy-start.66 = (f32[3072]{0:T(1024)S(1)}, f32[3072]{0:T(1024)}, u32[]{:S(2)}) copy-start(f32[3072]{0:T(1024)} %get-tuple-element.463) | copy-start | bytes 36868
  1047.0 324.5 %copy-start.48 = (f32[8832]{0:T(1024)S(1)}, f32[8832]{0:T(1024)}, u32[]{:S(2)}) copy-start(f32[8832]{0:T(1024)} %param.28) | copy-start | bytes 105988
  1047.0 324.5 %copy-start.55 = (f32[8832]{0:T(1024)S(1)}, f32[8832]{0:T(1024)}, u32[]{:S(2)}) copy-start(f32[8832]{0:T(1024)} %param.29) | copy-start | bytes 105988
  1317.6 54.6 %copy-start.19 = (f32[13,128,128]{2,1,0:T(8,128)S(1)}, f32[13,128,128]{2,1,0:T(8,128)}, u32[]{:S(2)}) copy-start(f32[13,128,128]{2,1,0:T(8,128)} %reduce-scatter.2.cloned.1.call-done) | copy-start | bytes 2555908
  1319.7 54.2 %copy-start.21 = (f32[13,128,128]{1,2,0:T(8,128)S(1)}, f32[13,128,128]{1,2,0:T(8,128)}, u32[]{:S(2)}) copy-start(f32[13,128,128]{1,2,0:T(8,128)} %copy.250) | copy-start | bytes 2555908
  (89 other events, 346.7 us)
Sparse Core Ops, SparseCore 0:
  11.5 103.4 all-gather.1
  1030.2 287.3 reduce-scatter.1
where the time goes:
time: 1410 us; the launch traced here: 1390 us
  waiting for transfers between devices  465 us (33%)
  matrix products  390 us (28%)
  local copies, waits for them, and re-layouts  260 us (18%)
  other arithmetic  182 us (13%)
  blocking collectives  46.8 us (3%)
  starting transfers between devices  18.8 us (1%)
  between operations  17.8 us (1%)
    reduce_scatter x1, waiting for transfers between devices, per_device(): lax.psum_scatter(grad_stack, ('dp', 'seq'), scatter_dimension=0, tiled=True)  268 us
    all_gather x1, waiting for transfers between devices, per_device(): lax.all_gather(master_tiles.astype(jnp.bfloat16), ('dp', 'seq'), axis=0,...  97.4 us
    dot_general x16, matrix products, one_block(): jnp.einsum('qhd,khd->hqk', query_rows, key_heads, preferred_element_type=...  78.9 us
    dot_general x8, matrix products, one_block(): jnp.einsum('qhd,khd->hqk', grad_rows, value_heads, preferred_element_type...  57.1 us
    convert_element_type x8, other arithmetic, one_block(): score_grad = (probs * (probs_grad - delta)).astype(jnp.bfloat16)  54.9 us
    reduce_sum x8, other arithmetic, one_block(): totals = jnp.sum(exponent, axis=-1, keepdims=True)  54.1 us
    dot_general x8, matrix products, one_block(): jnp.einsum('hqk,khd->qhd', weights, value_heads, preferred_element_type=j...  53.5 us
    all_to_all x1, waiting for transfers between devices, per_device(): lax.all_to_all(packed, 'seq', split_axis=3, concat_axis=2, tiled=True)  53.2 us
  transfers between devices with their start and end apart: 6, of which 5 were waited for; matrix products, arithmetic and copies ran while one was open for 7% of the time, Pallas kernels for 0%

commit v1 on v0

--- a/solution.py
+++ b/solution.py
@@ -18,6 +18,12 @@
 vector_rate = 0.1
 moment_eps = 1e-08
 masked_score = -1e30
+
+
+def stacked_exchange(block, axis, split, join):
+    pieces = jnp.split(block, lax.axis_size(axis), axis=split)
+    arrived = lax.all_to_all(jnp.stack(pieces), axis, 0, 0)
+    return jnp.concatenate(arrived, axis=join)
 
 
 def matrix_shapes():
@@ -268,13 +274,7 @@
     query_grad, key_grad, value_grad = lax.map(
         attend_backward, (head_data[0], head_data[1], head_data[2], grad_heads, log_sums, lengths)
     )
-    sent_back = lax.all_to_all(
-        jnp.stack([query_grad, key_grad, value_grad]),
-        "seq",
-        split_axis=2,
-        concat_axis=3,
-        tiled=True,
-    )
+    sent_back = stacked_exchange(jnp.stack([query_grad, key_grad, value_grad]), "seq", 2, 3)
     queries_grad = sent_back[0].reshape(-1, model_width)
     keys_grad = sent_back[1].reshape(-1, model_width)
     values_grad = sent_back[2].reshape(-1, model_width)

time: 1410 us -> 1340 us (0.950)
  local copies, waits for them, and re-layouts: 260 us -> 228 us
  waiting for transfers between devices: 465 us -> 447 us
    all_to_all x1, waiting for transfers between devices: 36.8 us -> 19.8 us  [stacked_exchange(): arrived = lax.all_to_all(jnp.stack(pieces), axis, 0, 0)]
    while x75 -> x72, local copies, waits for them, and re-layouts: 20.2 us -> 3.5 us  [the longest x3 16.8 us: per_device(): lax.map(attend_backward, (head_data[0], head_data[1], head_data[2], grad_...]
    all_to_all x1 -> x0, local copies, waits for them, and re-layouts: 16.2 us -> none  [per_device(): lax.all_to_all(jnp.stack([query_grad, key_grad, value_grad]), 'seq', spli...]
where the time goes in v1:
time: 1340 us; the launch traced here: 1330 us
  waiting for transfers between devices  447 us (33%)
  matrix products  382 us (29%)
  local copies, waits for them, and re-layouts  228 us (17%)
  other arithmetic  176 us (13%)
  blocking collectives  46.8 us (3%)
  starting transfers between devices  18.4 us (1%)
  between operations  18 us (1%)
    reduce_scatter x1, waiting for transfers between devices, per_device(): lax.psum_scatter(grad_stack, ('dp', 'seq'), scatter_dimension=0, tiled=True)  268 us
    all_gather x1, waiting for transfers between devices, per_device(): lax.all_gather(master_tiles.astype(jnp.bfloat16), ('dp', 'seq'), axis=0,...  97.4 us
    dot_general x16, matrix products, one_block(): jnp.einsum('qhd,khd->hqk', query_rows, key_heads, preferred_element_type=...  80.5 us
    dot_general x8, matrix products, one_block(): jnp.einsum('qhd,khd->hqk', grad_rows, value_heads, preferred_element_type...  57.8 us
    convert_element_type x8, other arithmetic, one_block(): score_grad = (probs * (probs_grad - delta)).astype(jnp.bfloat16)  54.9 us
    reduce_sum x8, other arithmetic, one_block(): totals = jnp.sum(exponent, axis=-1, keepdims=True)  54.1 us
    dot_general x8, matrix products, one_block(): jnp.einsum('hqk,khd->qhd', weights, value_heads, preferred_element_type=j...  53.5 us
    all_to_all x1, waiting for transfers between devices, per_device(): lax.all_to_all(packed, 'seq', split_axis=3, concat_axis=2, tiled=True)  53.2 us
  transfers between devices with their start and end apart: 6, of which 5 were waited for; matrix products, arithmetic and copies ran while one was open for 7% of the time, Pallas kernels for 0%

profile of v1, /device:TPU:0, one launch (start us, length us, event | category | flops | bytes accessed | tf_op | source)
XLA Modules:
  0.0 1329.2 jit_solution(3531026092134601013)
XLA Ops:
  17.5 97.4 %all-gather.2.cloned.1.call-done = bf16[416,128,128]{2,1,0:T(8,128)(2,1)} async-done(((bf16[13,128,128]{2,1,0:T(8,128)(2,1)}), bf16[416,128,128]{2,1,0:T(8,128)(2,1)}) %all-gather.2.cloned.1.call-update) | async-done | bytes 13631504 | tf_op jit(solution)/shard_map/all_gather | solution.py:210
  143.5 13.8 %maximum_maximum_fusion = bf16[3,2,512,768]{2,1,0,3:T(2,128)(2,1)} fusion(bf16[1,2,512,384]{2,1,0,3:T(2,128)(2,1)S(1)} %bitcast.423, bf16[1,2,512,384]{2,1,0,3:T(2,128)(2,1)} %copy.104, bf16[1,2,512,768]{2,1,0,3:T(2,128)(2,1)S(1)} %copy.106, bf16[1,2,512,768]{2,1,0,3:T(2,128)(2,1)} %copy.105), kind=kLoop, calls=%fused_computation.93 | loop fusion | flops 7077888 | bytes 9437184 | tf_op jit(solution)/shard_map/stack | solution.py:230
  163.2 53.2 %all-to-all-done = bf16[3,2,512,768]{2,1,0,3:T(2,128)(2,1)} async-done(((bf16[3,2,512,768]{2,1,0,3:T(2,128)(2,1)}), bf16[3,2,512,768]{2,1,0,3:T(2,128)(2,1)}, u32[]{:S(2)}, u32[]{:S(2)}) %all-to-all-start) | async-done | bytes 4718624 | tf_op jit(solution)/shard_map/all_to_all | solution.py:233
  242.4 199.3 %while.54 = (s32[]{:T(128)}, bf16[2,2048,192]{1,2,0:T(8,128)(2,1)}, f32[2,3,2048]{2,1,0:T(4,128)S(1)}, bf16[2,2048,192]{1,2,0:T(8,128)(2,1)}, bf16[2,2048,192]{1...) while((s32[]{:T(128)}, bf16[2,2048,192]{1,2,0:T(8,128)(2,1)}, ...), condition=%wide.region_7.8_spmd, body=%wide.region_2.7_spmd.sunk | while | flops 845251584 | bytes 53479908 | solution.py:234
  247.1 93.0 %while.57 = (s32[]{:T(128)}, bf16[4,512,3,64]{1,3,2,0:T(8,128)(2,1)S(1)}, f32[4,3,512]{2,1,0:T(4,128)S(1)}, s32[4]{0:T(128)S(1)}, s32[]{:T(128)}, /*index=5*/bf1...) while((s32[]{:T(128)}, ...), condition=%wide.region_6.6_spmd, body=%wide.region_3.5_spmd.sunk | while | flops 845251584 | bytes 43976908 | solution.py:134
  272.9 7.2 fusion.206
  319.4 7.2 fusion.206
  346.5 93.0 %while.57 = (s32[]{:T(128)}, bf16[4,512,3,64]{1,3,2,0:T(8,128)(2,1)S(1)}, f32[4,3,512]{2,1,0:T(4,128)S(1)}, s32[4]{0:T(128)S(1)}, s32[]{:T(128)}, /*index=5*/bf1...) while((s32[]{:T(128)}, ...), condition=%wide.region_6.6_spmd, body=%wide.region_3.5_spmd.sunk | while | flops 845251584 | bytes 43976908 | solution.py:134
  455.2 9.1 fusion.122
  481.0 10.4 copy.112
  496.9 12.5 fusion.54
  509.4 15.1 %convert_reduce_fusion = (f32[3072]{0:T(1024)}, bf16[1024,3072]{1,0:T(8,128)(2,1)S(1)}) fusion(f32[1024,3072]{1,0:T(8,128)} %get-tuple-element.433, f32[3072]{0:T(1024)S(1)} %copy-done.64, bf16[1024,768]{1,0:T(8,128)(2,1)S(1)} %bitcast.396, bf16[96,8,24,128]{3,2,1,0:T(8,128)(2,1)S(1)} %bitcast.415), kind=kOutput, calls=%fused_computation.82 | convolution fusion | flops 4904186880 | bytes 25190400 | tf_op jit(solution)/shard_map/dot_general | solution.py:80
  547.6 8.7 copy.138
  556.3 8.6 all-to-all-done.2
  570.9 278.0 %while.56 = (s32[]{:T(128)}, bf16[2,2048,192]{1,2,0:T(8,128)(2,1)}, bf16[2,2048,192]{1,2,0:T(8,128)(2,1)}, bf16[2,2048,192]{1,2,0:T(8,128)(2,1)}, bf16[2,2048,19...) while((s32[]{:T(128)}, bf16[2,2048,192]{1,2,0:T(8,128)(2,1)}, ...), condition=%wide.region_16.17_spmd, body=%wide.region_12.16_spmd.sunk | while | flops 2065499136 | bytes 171613168 | solution.py:274
  578.2 122.2 %while.58 = (s32[]{:T(128)}, f32[2048,3,64]{0,2,1:T(8,128)S(1)}, f32[2048,3,64]{0,2,1:T(8,128)}, bf16[4,512,3,64]{1,3,2,0:T(8,128)(2,1)}, s32[4]{0:T(128)S(1)}, ...) while((s32[]{:T(128)}, f32[2048,3,64]{0,2,1:T(8,128)S(1)}, ...), condition=%wide.region_15.15_spmd.clone, body=%wide.region_13.14_spmd.clone.sunk | while | flops 2064712704 | bytes 114546992 | solution.py:185
  716.9 122.1 %while.58 = (s32[]{:T(128)}, f32[2048,3,64]{0,2,1:T(8,128)S(1)}, f32[2048,3,64]{0,2,1:T(8,128)}, bf16[4,512,3,64]{1,3,2,0:T(8,128)(2,1)}, s32[4]{0:T(128)S(1)}, ...) while((s32[]{:T(128)}, f32[2048,3,64]{0,2,1:T(8,128)S(1)}, ...), condition=%wide.region_15.15_spmd.clone, body=%wide.region_13.14_spmd.clone.sunk | while | flops 2064712704 | bytes 114546992 | solution.py:185
  859.6 8.9 convolution_bitcast_fusion
  884.1 9.5 fusion.133
  893.6 19.8 %all-to-all-done.3 = bf16[4,3,2,512,192]{3,4,2,1,0:T(8,128)(2,1)} async-done(((bf16[4,3,2,512,192]{3,4,2,1,0:T(8,128)(2,1)}), bf16[4,3,2,512,192]{3,4,2,1,0:T(8,128)(2,1)}, u32[]{:S(2)}, u32[]{:S(2)}) %all-to-all-start.3) | async-done | bytes 4718624 | tf_op jit(solution)/shard_map/all_to_all | solution.py:25
  956.9 8.8 constant_dynamic-update-slice_fusion.5
  968.8 14.6 %add_convert_fusion = bf16[1024,768]{1,0:T(8,128)(2,1)} fusion(f32[1024,768]{1,0:T(8,128)} %copy-done.6, bf16[96,8,24,128]{3,2,1,0:T(8,128)(2,1)} %bitcast.412, f32[1024,3072]{1,0:T(8,128)} %get-tuple-element.433, f32[3072]{0:T(1024)S(1)} %copy-done.65, f32[768]{0:T(1024)S(1)} %copy-done.67), kind=kOutput, calls=%fused_computation.131 | convolution fusion | flops 4865654784 | bytes 22035456 | tf_op jit(solution)/shard_map/dot_general | solution.py:70
  985.5 268.4 %reduce-scatter.2.cloned.1.call-done = f32[13,128,128]{2,1,0:T(8,128)} async-done(((f32[416,128,128]{2,1,0:T(8,128)}), f32[13,128,128]{2,1,0:T(8,128)}) %reduce-scatter.2.cloned.1.call-update) | async-done | bytes 851984 | tf_op jit(solution)/shard_map/reduce_scatter | solution.py:314
  1259.1 46.8 %all-reduce = (f32[]{:T(128)}, f32[8832]{0:T(1024)S(1)}) all-reduce(f32[]{:T(128)} %multiply_reduce_fusion.6, f32[8832]{0:T(1024)S(1)} %constant_dynamic-update-slice_fusion.12), channel_id=1, replica_groups=mesh['dp'=8,'seq'=4] {'dp','seq'}, use_global_device_ids=true, to_apply=%region_21.22 | all-reduce | flops 8833 | bytes 70664 | tf_op jit(solution)/shard_map/psum | solution.py:315
  (541 shorter events, 678.6 us)
Async XLA Ops:
  7.2 1301.4 %copy-start = (f32[13,128,128]{2,1,0:T(8,128)S(1)}, f32[13,128,128]{2,1,0:T(8,128)}, u32[]{:S(2)}) copy-start(f32[13,128,128]{2,1,0:T(8,128)} %param.27) | copy-start | bytes 2555908
  7.2 107.7 %all-gather.2.cloned.1.call-start = ((), (), s32[]{:S(2)}) async-start(), calls=%async_computation.5 | async-start | bytes 14057472 | tf_op jit(solution)/shard_map/all_gather | solution.py:210
  157.3 59.1 %all-to-all-start = ((bf16[3,2,512,768]{2,1,0,3:T(2,128)(2,1)}), bf16[3,2,512,768]{2,1,0,3:T(2,128)(2,1)}, u32[]{:S(2)}, u32[]{:S(2)}) async-start(bf16[3,2,512,768]{2,1,0,3:T(2,128)(2,1)} %maximum_maximum_fusion), calls=%async_computation | async-start | bytes 9437184 | tf_op jit(solution)/shard_map/all_to_all | solution.py:233
  447.7 32.0 %all-to-all-start.1 = ((bf16[2,2048,192]{2,0,1:T(2,128)(2,1)}), bf16[2,2048,192]{2,0,1:T(2,128)(2,1)S(1)}, u32[]{:S(2)}, u32[]{:S(2)}) async-start(bf16[2,2048,192]{2,0,1:T(2,128)(2,1)} %copy.111), calls=%async_computation.1 | async-start | bytes 4194304 | tf_op jit(solution)/shard_map/all_to_all | solution.py:237
  481.0 12.4 copy-start.4
  481.0 12.4 copy-start.68
  495.2 35.6 %copy-start.6 = (f32[1024,768]{1,0:T(8,128)}, f32[1024,768]{1,0:T(8,128)S(1)}, u32[]{:S(2)}) copy-start(f32[1024,768]{1,0:T(8,128)S(1)} %get-tuple-element.429) | copy-start | bytes 9437188
  495.2 35.5 %copy-start.43 = (f32[1024]{0:T(1024)}, f32[1024]{0:T(1024)S(1)}, u32[]{:S(2)}) copy-start(f32[1024]{0:T(1024)S(1)} %broadcast_multiply_fusion.6) | copy-start | bytes 12292
  495.2 14.1 %slice-start.5 = ((s8[4718592]{0:T(1024)(128)(4,1)}), s8[4194304]{0:T(1024)(128)(4,1)S(1)}, s32[]{:S(2)}) async-start(s8[4718592]{0:T(1024)(128)(4,1)} %bitcast.413), calls=%async_computation.12 | async-start | bytes 8388608
  495.8 35.0 %copy-start.45 = (f32[1024]{0:T(1024)}, f32[1024]{0:T(1024)S(1)}, u32[]{:S(2)}) copy-start(f32[1024]{0:T(1024)S(1)} %add_rsqrt_fusion) | copy-start | bytes 12292
  496.9 12.5 copy-start.10
  496.9 12.5 slice-start.6
  540.4 24.5 %all-to-all-start.2 = ((bf16[2,512,768]{1,0,2:T(2,128)(2,1)}), bf16[2,512,768]{1,0,2:T(2,128)(2,1)}, u32[]{:S(2)}, u32[]{:S(2)}) async-start(bf16[2,512,768]{1,0,2:T(2,128)(2,1)} %copy.116), calls=%async_computation.2 | async-start | bytes 3145728 | tf_op jit(solution)/shard_map/all_to_all | solution.py:267
  854.6 58.8 %all-to-all-start.3 = ((bf16[4,3,2,512,192]{3,4,2,1,0:T(8,128)(2,1)}), bf16[4,3,2,512,192]{3,4,2,1,0:T(8,128)(2,1)}, u32[]{:S(2)}, u32[]{:S(2)}) async-start(bf16[4,3,2,512,192]{3,4,2,1,0:T(8,128)(2,1)} %pad_maximum_fusion.1), calls=%async_computation.3 | async-start | bytes 9437184 | tf_op jit(solution)/shard_map/all_to_all | solution.py:25
  859.5 394.4 %reduce-scatter.2.cloned.1.call-start = ((), (), s32[]{:S(2)}) async-start(), calls=%async_computation.6 | async-start | bytes 28114944 | tf_op jit(solution)/shard_map/reduce_scatter | solution.py:314
  968.7 16.5 %copy-start.70 = (f32[768]{0:T(1024)S(1)}, f32[768]{0:T(1024)}, u32[]{:S(2)}) copy-start(f32[768]{0:T(1024)} %get-tuple-element.300) | copy-start | bytes 9220
  968.7 16.5 %copy-start.69 = (f32[768]{0:T(1024)S(1)}, f32[768]{0:T(1024)}, u32[]{:S(2)}) copy-start(f32[768]{0:T(1024)} %get-tuple-element.306) | copy-start | bytes 9220
  968.7 16.6 %copy-start.61 = (f32[768]{0:T(1024)S(1)}, f32[768]{0:T(1024)}, u32[]{:S(2)}) copy-start(f32[768]{0:T(1024)} %get-tuple-element.387) | copy-start | bytes 9220
  968.7 16.6 %copy-start.60 = (f32[768]{0:T(1024)S(1)}, f32[768]{0:T(1024)}, u32[]{:S(2)}) copy-start(f32[768]{0:T(1024)} %get-tuple-element.385) | copy-start | bytes 9220
  968.7 16.8 %copy-start.66 = (f32[3072]{0:T(1024)S(1)}, f32[3072]{0:T(1024)}, u32[]{:S(2)}) copy-start(f32[3072]{0:T(1024)} %get-tuple-element.434) | copy-start | bytes 36868
  983.4 324.5 %copy-start.48 = (f32[8832]{0:T(1024)S(1)}, f32[8832]{0:T(1024)}, u32[]{:S(2)}) copy-start(f32[8832]{0:T(1024)} %param.28) | copy-start | bytes 105988
  983.4 324.5 %copy-start.55 = (f32[8832]{0:T(1024)S(1)}, f32[8832]{0:T(1024)}, u32[]{:S(2)}) copy-start(f32[8832]{0:T(1024)} %param.29) | copy-start | bytes 105988
  1253.9 54.6 %copy-start.19 = (f32[13,128,128]{2,1,0:T(8,128)S(1)}, f32[13,128,128]{2,1,0:T(8,128)}, u32[]{:S(2)}) copy-start(f32[13,128,128]{2,1,0:T(8,128)} %reduce-scatter.2.cloned.1.call-done) | copy-start | bytes 2555908
  1256.0 54.2 %copy-start.21 = (f32[13,128,128]{1,2,0:T(8,128)S(1)}, f32[13,128,128]{1,2,0:T(8,128)}, u32[]{:S(2)}) copy-start(f32[13,128,128]{1,2,0:T(8,128)} %copy.129) | copy-start | bytes 2555908
  (89 other events, 345.9 us)
Sparse Core Ops, SparseCore 0:
  11.5 103.4 all-gather.1
  966.5 287.3 reduce-scatter.1
